TPU v7x, 256 devices: a whole 4x4x8 slice. The times are simulated.
256 devices in a mesh: dp: 4 (over y), mp: 64 (over x, z, core).
Axes of the slice: x: 4, y: 4, z: 8, core: 2. Of those that a mesh axis runs over, the one named last changes fastest.
Arguments:
- inputs: bfloat16 [8, 256, 6144], P('dp', None, 'mp'), may hold values from -6 to 6
- cotangent: bfloat16 [8, 256, 6144], P('dp', None, 'mp'), may hold values from -6 to 6
- w_up: bfloat16 [6144, 24576], P('dp', 'mp'), may hold values from -0.078125 to 0.078125
- w_down: bfloat16 [24576, 6144], P('mp', 'dp'), may hold values from -0.0390625 to 0.0390625
- thresholds: float32 [2], replicated, may hold values from 23592.96 to 58982.4
Outputs:
- grad_up: float32 [6144, 24576], P('dp', 'mp')
- grad_down: float32 [24576, 6144], P('mp', 'dp')
- norms: float32 [8, 2], P('dp')
All inputs are finite; a program needn't handle non-finite values.
Results may differ from a plain program's by a relative error of at most 0.0085.
Values may be sent and summed in bfloat16 or wider, within the bound.
A program may use at most 128 MiB of HBM per device.

v0:
```python
import jax
import jax.numpy as jnp
from jax import lax
from jax.sharding import PartitionSpec as P

inv_root_two = 0.7071067811865476
inv_root_two_pi = 0.3989422804014327


def sent_to_all(shard, axis):
    copies = jnp.broadcast_to(shard, (lax.axis_size(axis), *shard.shape))
    return lax.all_to_all(copies, axis, split_axis=0, concat_axis=0, tiled=True)


def taken_together(shard, axis):
    return sent_to_all(shard, axis).sum(axis=0)


def packed_total(arrays, axis):
    line, at, outs = (jnp.concatenate([a.reshape(-1) for a in arrays]), 0, [])
    running = taken_together(line, axis)
    for a in arrays:
        outs.append(running[at : at + a.size].reshape(a.shape))
        at += a.size
    return tuple(outs)


def split_up(shard, dim, count):
    shape = shard.shape
    pieces = shard.reshape(*shape[:dim], count, shape[dim] // count, *shape[dim + 1 :])
    return jnp.moveaxis(pieces, dim, 0)


def sum_at_owner(shard, axis, dim):
    pieces = split_up(shard, dim, lax.axis_size(axis))
    arrived = lax.all_to_all(pieces, axis, split_axis=0, concat_axis=0, tiled=True)
    return arrived.astype(jnp.float32).sum(axis=0)


def normal_cdf(value):
    return 0.5 * (1.0 + lax.erf(value * inv_root_two))


def gram_of(array, images, patches):
    cube = array.reshape(images, patches, -1)
    return jnp.einsum("btd,bsd->bts", cube, cube, preferred_element_type=jnp.float32)


def on_device(inputs, cotangent, w_up, w_down, thresholds):
    images, patches, local_feats = inputs.shape
    count_rows = images * patches
    x_whole = lax.all_gather(inputs, "mp", axis=2, tiled=True).reshape(count_rows, -1)
    hidden_local = w_up.shape[1]
    columns = x_whole
    pre = jnp.dot(
        columns, lax.all_gather(w_up, "dp", axis=0, tiled=True), preferred_element_type=jnp.float32
    )
    act = (pre * normal_cdf(pre)).astype(jnp.bfloat16)
    dy_whole = lax.all_gather(cotangent, "mp", axis=2, tiled=True).reshape(count_rows, -1)
    columns = dy_whole
    dact = lax.dot_general(
        columns,
        lax.all_gather(w_down, "dp", axis=1, tiled=True),
        (((1,), (1,)), ((), ())),
        preferred_element_type=jnp.float32,
    )
    slope = normal_cdf(pre) + pre * jnp.exp(-0.5 * pre * pre) * inv_root_two_pi
    dpre = (dact * slope).astype(jnp.bfloat16)
    gram_dpre = gram_of(dpre, images, patches)
    gram_act = gram_of(act, images, patches)
    part_up = jnp.sum(gram_of(x_whole, images, patches) * gram_dpre, axis=(1, 2))
    part_down = jnp.sum(gram_act * gram_of(dy_whole, images, patches), axis=(1, 2))
    sq_up, sq_down = packed_total((part_up, part_down), "mp")
    norms = jnp.stack([jnp.sqrt(sq_up), jnp.sqrt(sq_down)], axis=1)
    factor = jnp.minimum(1.0, thresholds[None, :] / (norms + 1e-06))
    dpre_clip = (
        (
            factor[:, 0][:, None, None]
            * dpre.reshape(images, patches, hidden_local).astype(jnp.float32)
        )
        .astype(jnp.bfloat16)
        .reshape(count_rows, hidden_local)
    )
    cot_clip = (
        (factor[:, 1][:, None, None] * dy_whole.reshape(images, patches, -1).astype(jnp.float32))
        .astype(jnp.bfloat16)
        .reshape(count_rows, -1)
    )
    columns = x_whole
    grad_up = lax.psum_scatter(
        lax.dot_general(
            columns, dpre_clip, (((0,), (0,)), ((), ())), preferred_element_type=jnp.float32
        ).astype(jnp.bfloat16),
        "dp",
        scatter_dimension=0,
        tiled=True,
    ).astype(jnp.float32)
    down_full = lax.dot_general(
        act, cot_clip, (((0,), (0,)), ((), ())), preferred_element_type=jnp.float32
    )
    grad_down = sum_at_owner(down_full.astype(jnp.bfloat16), "dp", 1)
    return (grad_up, grad_down, norms)


def solution(mesh):
    in_specs = (P("dp", None, "mp"), P("dp", None, "mp"), P("dp", "mp"), P("mp", "dp"), P())
    out_specs = (P("dp", "mp"), P("mp", "dp"), P("dp", None))
    return jax.shard_map(
        on_device, mesh=mesh, in_specs=in_specs, out_specs=out_specs, check_vma=False
    )
```

profile of v0, /device:TPU:1, one launch (start us, length us, event | category | flops | bytes accessed | tf_op | source)
XLA Modules:
  0.0 445.1 jit_solution(11769768210793305239)
XLA Ops:
  7.2 0.7 all-gather.5.cloned.1.call-update
  7.9 0.7 all-gather.7.cloned.1.call-update
  8.7 0.7 all-gather.11.cloned.1.call-update
  9.4 0.5 all-gather.9.cloned.1.call-update
  10.0 85.6 %all-gather.5.cloned.1.call-done = bf16[2,256,6144]{1,2,0:T(8,128)(2,1)} async-done(((bf16[2,256,96]{1,2,0:T(8,128)(2,1)}), bf16[2,256,6144]{1,2,0:T(8,128)(2,1)}) %all-gather.5.cloned.1.call-update) | async-done | bytes 6291472 | tf_op jit(solution)/shard_map/all_gather | solution.py:52
  95.5 8.7 %copy.32 = bf16[2,256,6144]{2,1,0:T(8,128)(2,1)} copy(bf16[2,256,6144]{1,2,0:T(8,128)(2,1)} %all-gather.5.cloned.1.call-done) | data formatting | bytes 12582912 | tf_op jit(solution)/shard_map/all_gather | solution.py:52
  104.2 71.4 %all-gather.7.cloned.1.call-done = bf16[2,256,6144]{1,2,0:T(8,128)(2,1)} async-done(((bf16[2,256,96]{1,2,0:T(8,128)(2,1)}), bf16[2,256,6144]{1,2,0:T(8,128)(2,1)}) %all-gather.7.cloned.1.call-update) | async-done | bytes 6291472 | tf_op jit(solution)/shard_map/all_gather | solution.py:59
  175.6 8.7 %copy.31 = bf16[2,256,6144]{2,1,0:T(8,128)(2,1)} copy(bf16[2,256,6144]{1,2,0:T(8,128)(2,1)} %all-gather.7.cloned.1.call-done) | data formatting | bytes 12582912 | tf_op jit(solution)/shard_map/all_gather | solution.py:59
  184.3 44.5 %all-gather.11.cloned.1.call-done = bf16[6144,384]{1,0:T(8,128)(2,1)} async-done(((bf16[1536,384]{1,0:T(8,128)(2,1)}), bf16[6144,384]{1,0:T(8,128)(2,1)}) %all-gather.11.cloned.1.call-update) | async-done | bytes 4718608 | tf_op jit(solution)/shard_map/all_gather | solution.py:56
  228.8 7.0 %multiply_convert_fusion.2 = (bf16[512,384]{1,0:T(8,128)(2,1)S(1)}, f32[512,384]{1,0:T(8,128)S(1)}) fusion(bf16[512,6144]{1,0:T(8,128)(2,1)} %bitcast.47, bf16[6144,384]{1,0:T(8,128)(2,1)} %all-gather.11.cloned.1.call-done), kind=kOutput, calls=%fused_computation.18 | convolution fusion | flops 2416902144 | bytes 12189696 | tf_op jit(solution)/shard_map/dot_general | solution.py:55
  235.7 50.3 %all-gather.9.cloned.1.call-done = bf16[384,6144]{1,0:T(8,128)(2,1)} async-done(((bf16[384,1536]{1,0:T(8,128)(2,1)}), bf16[384,6144]{1,0:T(8,128)(2,1)}) %all-gather.9.cloned.1.call-update) | async-done | bytes 4718608 | tf_op jit(solution)/shard_map/all_gather | solution.py:63
  286.0 7.7 %fusion.1 = bf16[512,384]{1,0:T(8,128)(2,1)S(1)} fusion(bf16[512,6144]{1,0:T(8,128)(2,1)} %bitcast.46, bf16[384,6144]{1,0:T(8,128)(2,1)} %all-gather.9.cloned.1.call-done, f32[512,384]{1,0:T(8,128)S(1)} %get-tuple-element.25), kind=kOutput, calls=%fused_computation.7 | convolution fusion | flops 2417885184 | bytes 12189696 | tf_op jit(solution)/shard_map/dot_general | solution.py:61
  293.7 0.3 fusion.9
  294.0 0.3 fusion.10
  294.4 7.4 %fusion.2 = f32[2]{0:T(128)S(1)} fusion(f32[2,256,256]{2,1,0:T(8,128)S(1)} %fusion.9, bf16[2,256,6144]{1,2,0:T(8,128)(2,1)} %all-gather.5.cloned.1.call-done), kind=kOutput, calls=%fused_computation.11 | convolution fusion | flops 1610874880 | bytes 6815752 | tf_op jit(solution)/shard_map/btd,bsd->bts/dot_general | solution.py:46
  301.8 2.7 fusion.3
  304.6 0.6 broadcast_in_dim.4
  305.2 10.8 %all-to-all-start = ((f32[64,1,4]{2,1,0:T(1,128)}), f32[64,1,4]{2,1,0:T(1,128)S(1)}, u32[]{:S(2)}, u32[]{:S(2)}) async-start(f32[64,1,4]{2,1,0:T(1,128)} %broadcast_in_dim.4), calls=%async_computation | async-start | bytes 65536 | tf_op jit(solution)/shard_map/all_to_all | solution.py:12
  316.1 0.2 reduce-scatter.2.cloned.1.call-start
  316.3 0.2 copy.34
  316.5 8.8 %all-to-all-done = f32[64,1,4]{2,1,0:T(1,128)S(1)} async-done(((f32[64,1,4]{2,1,0:T(1,128)}), f32[64,1,4]{2,1,0:T(1,128)S(1)}, u32[]{:S(2)}, u32[]{:S(2)}) %all-to-all-start) | async-done | bytes 1056 | tf_op jit(solution)/shard_map/all_to_all | solution.py:12
  325.3 0.1 reduce_sum.38
  325.5 8.6 %fusion = bf16[6144,384]{0,1:T(8,128)(2,1)} fusion(bf16[2,256,6144]{1,2,0:T(8,128)(2,1)} %all-gather.5.cloned.1.call-done, bf16[2,256,384]{1,2,0:T(8,128)(2,1)S(1)} %copy.34, f32[2]{0:T(128)S(1)} %get-tuple-element.21), kind=kOutput, calls=%fused_computation.4 | convolution fusion | flops 2418868224 | bytes 11403272 | tf_op jit(solution)/shard_map/dot_general | solution.py:91
  334.2 7.5 %multiply_convert_fusion = bf16[2,256,6144]{1,2,0:T(8,128)(2,1)} fusion(bf16[2,256,6144]{1,2,0:T(8,128)(2,1)} %all-gather.7.cloned.1.call-done, f32[2]{0:T(128)S(1)} %get-tuple-element.20), kind=kLoop, calls=%fused_computation | loop fusion | flops 9437184 | bytes 12582920 | tf_op jit(solution)/shard_map/convert_element_type | solution.py:86
  341.7 8.7 %copy.35 = bf16[2,256,6144]{2,1,0:T(8,128)(2,1)} copy(bf16[2,256,6144]{1,2,0:T(8,128)(2,1)} %multiply_convert_fusion) | data formatting | bytes 12582912 | tf_op jit(solution)/shard_map/convert_element_type | solution.py:86
  350.4 5.4 %convolution_convert_fusion = bf16[384,6144]{1,0:T(8,128)(2,1)S(1)} fusion(bf16[512,384]{1,0:T(8,128)(2,1)S(1)} %get-tuple-element.24, bf16[512,6144]{1,0:T(8,128)(2,1)} %bitcast.43), kind=kOutput, calls=%fused_computation.3 | convolution fusion | flops 2418278400 | bytes 11403264 | tf_op jit(solution)/shard_map/dot_general | solution.py:98
  355.8 2.6 copy.44
  358.4 4.9 %all-to-all-start.1 = ((bf16[4,384,1536]{2,1,0:T(8,128)(2,1)}), bf16[4,384,1536]{2,1,0:T(8,128)(2,1)}, u32[]{:S(2)}, u32[]{:S(2)}) async-start(bf16[4,384,1536]{2,1,0:T(8,128)(2,1)} %bitcast.44), calls=%async_computation.2 | async-start | bytes 9437184 | tf_op jit(solution)/shard_map/all_to_all | solution.py:36
  363.3 0.6 copy.38
  364.0 67.2 %all-to-all-done.1 = bf16[4,384,1536]{2,1,0:T(8,128)(2,1)} async-done(((bf16[4,384,1536]{2,1,0:T(8,128)(2,1)}), bf16[4,384,1536]{2,1,0:T(8,128)(2,1)}, u32[]{:S(2)}, u32[]{:S(2)}) %all-to-all-start.1) | async-done | bytes 4718624 | tf_op jit(solution)/shard_map/all_to_all | solution.py:36
  431.2 4.7 %convert_reduce_fusion = f32[384,1536]{1,0:T(8,128)} fusion(bf16[4,384,1536]{2,1,0:T(8,128)(2,1)} %all-to-all-done.1), kind=kLoop, calls=%fused_computation.2 | loop fusion | flops 4128768 | bytes 7077888 | tf_op jit(solution)/shard_map/reduce_sum | solution.py:37
  435.9 2.7 copy.37
  (17 shorter events, 0.4 us)
Async XLA Ops:
  7.2 88.4 %all-gather.5.cloned.1.call-start = ((), (), s32[]{:S(2)}) async-start(), calls=%async_computation.3 | async-start | bytes 6389760 | tf_op jit(solution)/shard_map/all_gather | solution.py:52
  7.9 167.7 %all-gather.7.cloned.1.call-start = ((), (), s32[]{:S(2)}) async-start(), calls=%async_computation.4 | async-start | bytes 6389760 | tf_op jit(solution)/shard_map/all_gather | solution.py:59
  8.6 220.1 %all-gather.11.cloned.1.call-start = ((), (), s32[]{:S(2)}) async-start(), calls=%async_computation.6 | async-start | bytes 5898240 | tf_op jit(solution)/shard_map/all_gather | solution.py:56
  9.4 276.6 %all-gather.9.cloned.1.call-start = ((), (), s32[]{:S(2)}) async-start(), calls=%async_computation.5 | async-start | bytes 5898240 | tf_op jit(solution)/shard_map/all_gather | solution.py:63
  294.0 7.8 %slice-start = ((s8[6291456]{0:T(1024)(128)(4,1)}), s8[4194304]{0:T(1024)(128)(4,1)S(1)}, s32[]{:S(2)}) async-start(s8[6291456]{0:T(1024)(128)(4,1)} %bitcast.41), calls=%async_computation.8 | async-start | bytes 8388608
  294.4 7.4 %slice-start.1 = ((s8[6291456]{0:T(1024)(128)(4,1)}), s8[2097152]{0:T(1024)(128)(4,1)S(1)}, s32[]{:S(2)}) async-start(s8[6291456]{0:T(1024)(128)(4,1)} %bitcast.41), calls=%async_computation.9 | async-start | bytes 4194304
  301.8 23.7 %copy-start = (f32[2]{0:T(128)S(1)}, f32[2]{0:T(128)}, u32[]{:S(2)}) copy-start(f32[2]{0:T(128)} %param.9) | copy-start | bytes 28
  305.2 20.1 %all-to-all-start = ((f32[64,1,4]{2,1,0:T(1,128)}), f32[64,1,4]{2,1,0:T(1,128)S(1)}, u32[]{:S(2)}, u32[]{:S(2)}) async-start(f32[64,1,4]{2,1,0:T(1,128)} %broadcast_in_dim.4), calls=%async_computation | async-start | bytes 65536 | tf_op jit(solution)/shard_map/all_to_all | solution.py:12
  316.1 119.8 %reduce-scatter.2.cloned.1.call-start = ((), (), s32[]{:S(2)}) async-start(), calls=%async_computation.7 | async-start | bytes 5898240 | tf_op jit(solution)/shard_map/reduce_scatter | solution.py:90
  358.4 72.8 %all-to-all-start.1 = ((bf16[4,384,1536]{2,1,0:T(8,128)(2,1)}), bf16[4,384,1536]{2,1,0:T(8,128)(2,1)}, u32[]{:S(2)}, u32[]{:S(2)}) async-start(bf16[4,384,1536]{2,1,0:T(8,128)(2,1)} %bitcast.44), calls=%async_computation.2 | async-start | bytes 9437184 | tf_op jit(solution)/shard_map/all_to_all | solution.py:36
Sparse Core Ops, SparseCore 0:
  10.8 84.6 all-gather.4
  98.3 77.2 all-gather.6
  177.4 51.2 all-gather.10
  230.4 55.5 all-gather.8
  334.3 59.8 reduce-scatter.1
where the time goes:
time: 446 us; the launch traced here: 445 us
  waiting for transfers between devices  330 us (74%)
  matrix products  39.5 us (9%)
  local copies, waits for them, and re-layouts  32.9 us (7%)
  starting transfers between devices  16.1 us (4%)
  between operations  13.9 us (3%)
  other arithmetic  12.4 us (3%)
    all_gather x1, waiting for transfers between devices, on_device(): lax.all_gather(inputs, 'mp', axis=2, tiled=True).reshape(count_rows, -1)  85.6 us
    all_gather x1, waiting for transfers between devices, on_device(): lax.all_gather(cotangent, 'mp', axis=2, tiled=True).reshape(count_rows, -1)  71.4 us
    all_to_all x1, waiting for transfers between devices, sum_at_owner(): lax.all_to_all(pieces, axis, split_axis=0, concat_axis=0, tiled=True)  67.2 us
    all_gather x1, waiting for transfers between devices, on_device(): lax.all_gather(w_down, 'dp', axis=1, tiled=True)  50.3 us
    all_gather x1, waiting for transfers between devices, on_device(): lax.all_gather(w_up, 'dp', axis=0, tiled=True)  44.5 us
    all_to_all x1, starting transfers between devices, sent_to_all(): return lax.all_to_all(copies, axis, split_axis=0, concat_axis=0, tiled=True)  10.8 us
    dot_general x4, matrix products, gram_of(): jnp.einsum('btd,bsd->bts', cube, cube, preferred_element_type=jnp.float32)  10.8 us
  transfers between devices with their start and end apart: 7, of which 6 were waited for; matrix products, arithmetic and copies ran while one was open for 12% of the time, Pallas kernels for 0%

commit v1 on v0

--- a/solution.py
+++ b/solution.py
@@ -5,6 +5,28 @@
 
 inv_root_two = 0.7071067811865476
 inv_root_two_pi = 0.3989422804014327
+
+
+def joined_along(blocks, dim):
+    blocks = jnp.moveaxis(blocks, 0, dim)
+    shape = blocks.shape
+    return blocks.reshape(*shape[:dim], shape[dim] * shape[dim + 1], *shape[dim + 2 :])
+
+
+def ring_gather(x, axis, dim):
+    devices = lax.axis_size(axis)
+    pairs = [(i, (i + 1) % devices) for i in range(devices)]
+    back = [(b, a) for a, b in pairs]
+    lower, upper = ([], [])
+    for step in range(devices - 1):
+        if step % 2 == 0:
+            lower.append(lax.ppermute(lower[-1] if lower else x, axis, pairs))
+        else:
+            upper.append(lax.ppermute(upper[-1] if upper else x, axis, back))
+    parts = jnp.stack([*lower[::-1], x, *upper])
+    shift = lax.axis_index(axis) - len(lower)
+    parts = parts[(jnp.arange(devices) - shift) % devices]
+    return joined_along(parts, dim)
 
 
 def sent_to_all(shard, axis):
@@ -60,7 +82,7 @@
     columns = dy_whole
     dact = lax.dot_general(
         columns,
-        lax.all_gather(w_down, "dp", axis=1, tiled=True),
+        ring_gather(w_down, "dp", 1),
         (((1,), (1,)), ((), ())),
         preferred_element_type=jnp.float32,
     )

time: 446 us -> 391 us (0.88)
  waiting for transfers between devices: 330 us -> 250 us
  blocking collectives: 0 us -> 20.2 us
  local copies, waits for them, and re-layouts: 32.9 us -> 44.5 us
  starting transfers between devices: 16.1 us -> 10.3 us
    all_gather x1, waiting for transfers between devices: 85.6 us -> 16.2 us  [on_device(): lax.all_gather(inputs, 'mp', axis=2, tiled=True).reshape(count_rows, -1)]
    all_gather x1 -> x0, waiting for transfers between devices: 50.3 us -> none  [on_device(): lax.all_gather(w_down, 'dp', axis=1, tiled=True)]
    ppermute x0 -> x3, waiting for transfers between devices: none -> 48.7 us  [the longest x2 48.7 us: ring_gather(): lower.append(lax.ppermute(lower[-1] if lower else x, axis, pairs))]
    all_to_all x0 -> x1, blocking collectives: none -> 20.2 us  [sent_to_all(): return lax.all_to_all(copies, axis, split_axis=0, concat_axis=0, tiled=True)]
    all_to_all x1 -> x0, starting transfers between devices: 10.8 us -> none  [sent_to_all(): return lax.all_to_all(copies, axis, split_axis=0, concat_axis=0, tiled=True)]
    all_to_all x1 -> x0, waiting for transfers between devices: 8.83 us -> none  [sent_to_all(): return lax.all_to_all(copies, axis, split_axis=0, concat_axis=0, tiled=True)]
    transpose x0 -> x1, local copies, waits for them, and re-layouts: none -> 6.8 us  [joined_along(): blocks = jnp.moveaxis(blocks, 0, dim)]
    gather x0 -> x1, local copies, waits for them, and re-layouts: none -> 5.35 us  [ring_gather(): parts = parts[(jnp.arange(devices) - shift) % devices]]
  transfers between devices with their start and end apart: 7 -> 8, of which waited for: 6 -> 6; matrix products, arithmetic and copies ran while one was open for 12% -> 16% of each run, Pallas kernels for 0% -> 0%
where the time goes in v1:
time: 391 us; the launch traced here: 390 us
  waiting for transfers between devices  250 us (64%)
  local copies, waits for them, and re-layouts  44.5 us (11%)
  matrix products  35.1 us (9%)
  blocking collectives  20.2 us (5%)
  other arithmetic  16.1 us (4%)
  between operations  13.9 us (4%)
  starting transfers between devices  10.3 us (3%)
    all_gather x1, waiting for transfers between devices, on_device(): lax.all_gather(cotangent, 'mp', axis=2, tiled=True).reshape(count_rows, -1)  71.4 us
    all_to_all x1, waiting for transfers between devices, sum_at_owner(): lax.all_to_all(pieces, axis, split_axis=0, concat_axis=0, tiled=True)  67.1 us
    ppermute x2, waiting for transfers between devices, ring_gather(): lower.append(lax.ppermute(lower[-1] if lower else x, axis, pairs))  48.7 us
    all_gather x1, waiting for transfers between devices, on_device(): lax.all_gather(w_up, 'dp', axis=0, tiled=True)  44.3 us
    all_to_all x1, blocking collectives, sent_to_all(): return lax.all_to_all(copies, axis, split_axis=0, concat_axis=0, tiled=True)  20.2 us
    all_gather x1, waiting for transfers between devices, on_device(): lax.all_gather(inputs, 'mp', axis=2, tiled=True).reshape(count_rows, -1)  16.2 us
    dot_general x4, matrix products, gram_of(): jnp.einsum('btd,bsd->bts', cube, cube, preferred_element_type=jnp.float32)  10.8 us
    all_gather x1, local copies, waits for them, and re-layouts, on_device(): lax.all_gather(cotangent, 'mp', axis=2, tiled=True).reshape(count_rows, -1)  8.81 us
  transfers between devices with their start and end apart: 8, of which 6 were waited for; matrix products, arithmetic and copies ran while one was open for 16% of the time, Pallas kernels for 0%

profile of v1, /device:TPU:1, one launch (start us, length us, event | category | flops | bytes accessed | tf_op | source)
XLA Modules:
  0.0 390.1 jit_solution(6424586535182206242)
XLA Ops:
  7.2 0.7 all-gather.4.cloned.1.call-update
  7.9 0.7 all-gather.6.cloned.1.call-update
  8.7 0.7 all-gather.8.cloned.1.call-update
  9.4 2.2 collective-permute-start
  11.6 1.5 collective-permute-start.2
  13.2 24.0 %collective-permute-done = bf16[384,1536]{1,0:T(8,128)(2,1)S(1)} collective-permute-done((bf16[384,1536]{1,0:T(8,128)(2,1)}, bf16[384,1536]{1,0:T(8,128)(2,1)S(1)}, u32[]{:S(2)}, u32[]{:S(2)}) %collective-permute-start) | collective-permute-done | bytes 1179680 | tf_op jit(solution)/shard_map/ppermute | solution.py:23
  37.1 1.5 collective-permute-start.1
  38.7 24.8 %collective-permute-done.1 = bf16[384,1536]{1,0:T(8,128)(2,1)S(1)} collective-permute-done((bf16[384,1536]{1,0:T(8,128)(2,1)S(1)}, bf16[384,1536]{1,0:T(8,128)(2,1)S(1)}, u32[]{:S(2)}, u32[]{:S(2)}) %collective-permute-start.1) | collective-permute-done | bytes 1179680 | tf_op jit(solution)/shard_map/ppermute | solution.py:23
  63.4 3.7 pad_maximum_fusion
  67.1 5.4 %gather_fusion = bf16[4,384,1536]{2,1,0:T(8,128)(2,1)} fusion(bf16[4,384,1536]{2,1,0:T(8,128)(2,1)} %pad_maximum_fusion, s32[1024]{0:T(1024)S(1)} %pad_clamp_fusion), kind=kCustom, calls=%fused_computation | custom fusion | bytes 9437200 | tf_op jit(solution)/shard_map/gather | solution.py:28
  72.5 6.8 %copy.85 = bf16[384,4,1536]{0,2,1:T(8,128)(2,1)} copy(bf16[384,4,1536]{2,0,1:T(8,128)(2,1)} %bitcast.63) | data formatting | bytes 9437184 | tf_op jit(solution)/shard_map/transpose | solution.py:11
  79.3 16.2 %all-gather.4.cloned.1.call-done = bf16[2,256,6144]{1,2,0:T(8,128)(2,1)} async-done(((bf16[2,256,96]{1,2,0:T(8,128)(2,1)}), bf16[2,256,6144]{1,2,0:T(8,128)(2,1)}) %all-gather.4.cloned.1.call-update) | async-done | bytes 6291472 | tf_op jit(solution)/shard_map/all_gather | solution.py:74
  95.5 8.7 %copy.87 = bf16[2,256,6144]{2,1,0:T(8,128)(2,1)} copy(bf16[2,256,6144]{1,2,0:T(8,128)(2,1)} %all-gather.4.cloned.1.call-done) | data formatting | bytes 12582912 | tf_op jit(solution)/shard_map/all_gather | solution.py:74
  104.2 71.4 %all-gather.6.cloned.1.call-done = bf16[2,256,6144]{1,2,0:T(8,128)(2,1)} async-done(((bf16[2,256,96]{1,2,0:T(8,128)(2,1)}), bf16[2,256,6144]{1,2,0:T(8,128)(2,1)}) %all-gather.6.cloned.1.call-update) | async-done | bytes 6291472 | tf_op jit(solution)/shard_map/all_gather | solution.py:81
  175.6 8.8 %copy.86 = bf16[2,256,6144]{2,1,0:T(8,128)(2,1)} copy(bf16[2,256,6144]{1,2,0:T(8,128)(2,1)} %all-gather.6.cloned.1.call-done) | data formatting | bytes 12582912 | tf_op jit(solution)/shard_map/all_gather | solution.py:81
  184.4 44.3 %all-gather.8.cloned.1.call-done = bf16[6144,384]{1,0:T(8,128)(2,1)} async-done(((bf16[1536,384]{1,0:T(8,128)(2,1)}), bf16[6144,384]{1,0:T(8,128)(2,1)}) %all-gather.8.cloned.1.call-update) | async-done | bytes 4718608 | tf_op jit(solution)/shard_map/all_gather | solution.py:78
  228.8 7.2 %multiply_convert_fusion.2 = (bf16[512,384]{0,1:T(8,128)(2,1)S(1)}, f32[512,384]{0,1:T(8,128)S(1)}) fusion(bf16[512,6144]{1,0:T(8,128)(2,1)} %bitcast.64, bf16[6144,384]{1,0:T(8,128)(2,1)} %all-gather.8.cloned.1.call-done), kind=kOutput, calls=%fused_computation.21 | convolution fusion | flops 2416902144 | bytes 12189696 | tf_op jit(solution)/shard_map/dot_general | solution.py:77
  236.0 2.9 fusion.2
  238.9 0.3 fusion.9
  239.8 7.4 %fusion.3 = f32[2]{0:T(128)S(1)} fusion(f32[2,256,256]{2,1,0:T(8,128)S(1)} %fusion.9, bf16[2,256,6144]{1,2,0:T(8,128)(2,1)} %all-gather.4.cloned.1.call-done), kind=kOutput, calls=%fused_computation.14 | convolution fusion | flops 1610874880 | bytes 6815752 | tf_op jit(solution)/shard_map/btd,bsd->bts/dot_general | solution.py:68
  247.3 2.7 fusion.4
  250.1 20.2 %all_to_all.11 = f32[64,1,4]{2,1,0:T(1,128)S(1)} all-to-all(f32[64,1,4]{2,1,0:T(1,128)S(1)} %broadcast_in_dim.2), channel_id=1, replica_groups=mesh['dp'=4,'mp'=64] {'mp'}, dimensions={0} | all-to-all | bytes 2048 | tf_op jit(solution)/shard_map/all_to_all | solution.py:34
  270.5 8.6 %fusion = bf16[6144,384]{0,1:T(8,128)(2,1)} fusion(bf16[2,256,6144]{1,2,0:T(8,128)(2,1)} %all-gather.4.cloned.1.call-done, f32[2]{0:T(128)S(1)} %get-tuple-element.24, bf16[48,2,8,256]{3,2,1,0:T(8,128)(2,1)S(1)} %bitcast.77), kind=kOutput, calls=%fused_computation.5 | convolution fusion | flops 2418868224 | bytes 11403272 | tf_op jit(solution)/shard_map/dot_general | solution.py:113
  279.1 7.5 %multiply_convert_fusion = bf16[2,256,6144]{1,2,0:T(8,128)(2,1)} fusion(bf16[2,256,6144]{1,2,0:T(8,128)(2,1)} %all-gather.6.cloned.1.call-done, f32[2]{0:T(128)S(1)} %get-tuple-element.23), kind=kLoop, calls=%fused_computation.1 | loop fusion | flops 9437184 | bytes 12582920 | tf_op jit(solution)/shard_map/convert_element_type | solution.py:108
  286.6 8.7 %copy.99 = bf16[2,256,6144]{2,1,0:T(8,128)(2,1)} copy(bf16[2,256,6144]{1,2,0:T(8,128)(2,1)} %multiply_convert_fusion) | data formatting | bytes 12582912 | tf_op jit(solution)/shard_map/convert_element_type | solution.py:108
  295.3 5.6 %convolution_convert_fusion = bf16[384,6144]{1,0:T(8,128)(2,1)S(1)} fusion(bf16[512,384]{0,1:T(8,128)(2,1)S(1)} %get-tuple-element.27, bf16[512,6144]{1,0:T(8,128)(2,1)} %bitcast.66), kind=kOutput, calls=%fused_computation.4 | convolution fusion | flops 2418278400 | bytes 11403264 | tf_op jit(solution)/shard_map/dot_general | solution.py:120
  300.9 2.5 copy.119
  303.5 5.0 %all-to-all-start.1 = ((bf16[4,384,1536]{2,1,0:T(8,128)(2,1)}), bf16[4,384,1536]{2,1,0:T(8,128)(2,1)}, u32[]{:S(2)}, u32[]{:S(2)}) async-start(bf16[4,384,1536]{2,1,0:T(8,128)(2,1)} %bitcast.62), calls=%async_computation.2 | async-start | bytes 9437184 | tf_op jit(solution)/shard_map/all_to_all | solution.py:58
  308.4 0.6 copy.102
  309.1 67.1 %all-to-all-done.1 = bf16[4,384,1536]{2,1,0:T(8,128)(2,1)} async-done(((bf16[4,384,1536]{2,1,0:T(8,128)(2,1)}), bf16[4,384,1536]{2,1,0:T(8,128)(2,1)}, u32[]{:S(2)}, u32[]{:S(2)}) %all-to-all-start.1) | async-done | bytes 4718624 | tf_op jit(solution)/shard_map/all_to_all | solution.py:58
  376.1 4.7 %convert_reduce_fusion = f32[384,1536]{1,0:T(8,128)} fusion(bf16[4,384,1536]{2,1,0:T(8,128)(2,1)} %all-to-all-done.1), kind=kLoop, calls=%fused_computation.3 | loop fusion | flops 4128768 | bytes 7077888 | tf_op jit(solution)/shard_map/reduce_sum | solution.py:59
  380.8 2.7 copy.101
  (31 shorter events, 1.1 us)
Async XLA Ops:
  7.2 88.4 %all-gather.4.cloned.1.call-start = ((), (), s32[]{:S(2)}) async-start(), calls=%async_computation.3 | async-start | bytes 6389760 | tf_op jit(solution)/shard_map/all_gather | solution.py:74
  7.9 167.7 %all-gather.6.cloned.1.call-start = ((), (), s32[]{:S(2)}) async-start(), calls=%async_computation.4 | async-start | bytes 6389760 | tf_op jit(solution)/shard_map/all_gather | solution.py:81
  8.6 220.1 %all-gather.8.cloned.1.call-start = ((), (), s32[]{:S(2)}) async-start(), calls=%async_computation.5 | async-start | bytes 5898240 | tf_op jit(solution)/shard_map/all_gather | solution.py:78
  9.4 371.4 %reduce-scatter.2.cloned.1.call-start = ((), (), s32[]{:S(2)}) async-start(), calls=%async_computation.6 | async-start | bytes 5898240 | tf_op jit(solution)/shard_map/reduce_scatter | solution.py:112
  9.4 27.7 %collective-permute-start = (bf16[384,1536]{1,0:T(8,128)(2,1)}, bf16[384,1536]{1,0:T(8,128)(2,1)S(1)}, u32[]{:S(2)}, u32[]{:S(2)}) collective-permute-start(bf16[384,1536]{1,0:T(8,128)(2,1)} %param.8), channel_id=1, source_target_pairs={{0,64},{64,128},{128,192},{192,0},{1,65},{65,129},{129,193},{193,1... | collective-permute-start | bytes 3538952 | tf_op jit(solution)/shard_map/ppermute | solution.py:23
  11.6 27.1 %collective-permute-start.2 = (bf16[384,1536]{1,0:T(8,128)(2,1)}, bf16[384,1536]{1,0:T(8,128)(2,1)S(1)}, u32[]{:S(2)}, u32[]{:S(2)}) collective-permute-start(bf16[384,1536]{1,0:T(8,128)(2,1)} %param.8), channel_id=1, source_target_pairs={{64,0},{128,64},{192,128},{0,192},{65,1},{129,65},{193,129},{1,193... | collective-permute-start | bytes 3538952 | tf_op jit(solution)/shard_map/ppermute | solution.py:25
  37.1 26.3 %collective-permute-start.1 = (bf16[384,1536]{1,0:T(8,128)(2,1)S(1)}, bf16[384,1536]{1,0:T(8,128)(2,1)S(1)}, u32[]{:S(2)}, u32[]{:S(2)}) collective-permute-start(bf16[384,1536]{1,0:T(8,128)(2,1)S(1)} %collective-permute-done), channel_id=1, source_target_pairs={{0,64},{64,128},{128,192},{192,0},{1,65},{65,129},{129,193},{193,1... | collective-permute-start | bytes 3538952 | tf_op jit(solution)/shard_map/ppermute | solution.py:23
  175.6 60.4 %slice-start.2 = ((s8[4718592]{0:T(1024)(128)(4,1)}), s8[524288]{0:T(1024)(128)(4,1)S(1)}, s32[]{:S(2)}) async-start(s8[4718592]{0:T(1024)(128)(4,1)} %bitcast.67), calls=%async_computation.9 | async-start | bytes 1048576
  228.8 7.2 %copy-start = (bf16[2,256,6144]{2,1,0:T(8,128)(2,1)S(1)}, bf16[2,256,6144]{2,1,0:T(8,128)(2,1)}, u32[]{:S(2)}) copy-start(bf16[2,256,6144]{2,1,0:T(8,128)(2,1)} %copy.86) | copy-start | bytes 18874372
  228.8 7.2 %slice-start.3 = ((s8[4718592]{0:T(1024)(128)(4,1)}), s8[4194304]{0:T(1024)(128)(4,1)S(1)}, s32[]{:S(2)}) async-start(s8[4718592]{0:T(1024)(128)(4,1)} %bitcast.67), calls=%async_computation.10 | async-start | bytes 8388608
  239.5 7.8 %slice-start = ((s8[6291456]{0:T(1024)(128)(4,1)}), s8[4194304]{0:T(1024)(128)(4,1)S(1)}, s32[]{:S(2)}) async-start(s8[6291456]{0:T(1024)(128)(4,1)} %bitcast.60), calls=%async_computation.7 | async-start | bytes 8388608
  239.8 7.4 %slice-start.1 = ((s8[6291456]{0:T(1024)(128)(4,1)}), s8[2097152]{0:T(1024)(128)(4,1)S(1)}, s32[]{:S(2)}) async-start(s8[6291456]{0:T(1024)(128)(4,1)} %bitcast.60), calls=%async_computation.8 | async-start | bytes 4194304
  247.3 23.1 %copy-start.1 = (f32[2]{0:T(128)S(1)}, f32[2]{0:T(128)}, u32[]{:S(2)}) copy-start(f32[2]{0:T(128)} %param.9) | copy-start | bytes 28
  303.5 72.7 %all-to-all-start.1 = ((bf16[4,384,1536]{2,1,0:T(8,128)(2,1)}), bf16[4,384,1536]{2,1,0:T(8,128)(2,1)}, u32[]{:S(2)}, u32[]{:S(2)}) async-start(bf16[4,384,1536]{2,1,0:T(8,128)(2,1)} %bitcast.62), calls=%async_computation.2 | async-start | bytes 9437184 | tf_op jit(solution)/shard_map/all_to_all | solution.py:58
Sparse Core Ops, SparseCore 0:
  10.8 84.6 all-gather.3
  98.3 77.2 all-gather.5
  177.4 51.2 all-gather.7
  279.2 59.6 reduce-scatter.1
